TPU v7x, 512 devices: a whole 4x4x16 slice. The times are simulated.
512 devices in a mesh: seq: 64 (over y, z_lo, x), tp: 8 (over z_hi, core).
Axes of the slice: x: 4, y: 4, z: 16 (z_hi: 4, z_lo: 4; z = z_hi * 4 + z_lo), core: 2. Of those that a mesh axis runs over, the one named last changes fastest.
Arguments:
- video_tokens: bfloat16 [8192, 5120], P('seq'), may hold values from -40 to 40
- w_query: bfloat16 [5120, 5120], P('seq', 'tp'), may hold values from -1 to 1
- text_keys: bfloat16 [128, 5120], P(None, 'tp'), may hold values from -4 to 4
- text_values: bfloat16 [128, 5120], P(None, 'tp'), may hold values from -4 to 4
- grad_out: bfloat16 [8192, 5120], P('seq', 'tp'), may hold values from -5 to 5
Outputs:
- grad_video: bfloat16 [8192, 5120], P(('seq', 'tp'))
- grad_keys: bfloat16 [128, 5120], P('seq', 'tp')
- grad_values: bfloat16 [128, 5120], P('seq', 'tp')
All inputs are finite; a program needn't handle non-finite values.
Results may differ from a plain program's by a relative error of at most 0.014.
Values may be sent and summed in bfloat16 or wider, within the bound.
A program may use at most 64 MiB of HBM per device.

v0:
```python
import jax
import jax.numpy as jnp
from jax import lax
from jax.sharding import Mesh
from jax.sharding import PartitionSpec as P

HEAD_DIM = 128
SEQ = ("seq_0", "seq_1", "seq_2")
SEQ_TP = ("seq_0", "seq_1", "seq_2", "tp")


def laid_out(tiles, dim):
    dims = list(tiles.shape[1:])
    dims[dim] *= tiles.shape[0]
    return jnp.moveaxis(tiles, 0, dim).reshape(dims)


def all_blocks(x, axes, turns):
    tiles = x
    for k in turns:
        tiles = lax.all_gather(tiles, axes[k])
    done = turns[::-1]
    back = [done.index(k) for k in range(len(axes))]
    tiles = tiles.transpose(*back, *range(len(axes), tiles.ndim))
    return tiles.reshape(-1, *x.shape)


def gather_axes(x, axes, turns, dim):
    return laid_out(all_blocks(x, axes, turns), dim)


def split_up(x, dim, length):
    before, after = (x.shape[:dim], x.shape[dim + 1 :])
    return jnp.moveaxis(x.reshape(*before, length, -1, *after), dim, 0)


def sum_at_owner(x, axis, dim):
    length = lax.axis_size(axis)
    tiles = lax.all_to_all(split_up(x, dim, length), axis, 0, 0, tiled=True)
    return jnp.sum(tiles, axis=0)


def sent_together(arrays, axis, dim, along):
    widths = [a.shape[along] for a in arrays]
    both = jnp.concatenate(arrays, axis=along)
    result = sum_at_owner(both, axis, dim)
    return tuple(jnp.split(result, [sum(widths[:k]) for k in range(1, len(widths))], axis=along))


def summed_on_arrival(x, axis, dim):
    length = lax.axis_size(axis)
    tiles = lax.all_to_all(split_up(x, dim, length), axis, 0, 0, tiled=True)
    return jnp.sum(tiles.astype(jnp.float32), axis=0)


def local(video_tokens, w_query, text_keys, text_values, grad_out):
    factor = HEAD_DIM ** (-0.5)
    tokens_here = video_tokens.shape[0]
    text_len = text_keys.shape[0]
    heads_here = text_keys.shape[1] // HEAD_DIM
    gathered = gather_axes(w_query, SEQ, (1, 0, 2), 0)
    query = jnp.dot(video_tokens, gathered, preferred_element_type=jnp.float32).astype(jnp.bfloat16)
    query_heads = query.reshape(tokens_here, heads_here, HEAD_DIM)
    key_heads = text_keys.reshape(text_len, heads_here, HEAD_DIM)
    value_heads = text_values.reshape(text_len, heads_here, HEAD_DIM)
    grad_heads = grad_out.reshape(tokens_here, heads_here, HEAD_DIM)
    scores = (
        jnp.einsum("thd,lhd->thl", query_heads, key_heads, preferred_element_type=jnp.float32)
        * factor
    )
    row_max = jnp.max(scores, axis=2, keepdims=True)
    raised = jnp.exp(scores - row_max)
    attend = raised / jnp.sum(raised, axis=2, keepdims=True)
    attend_half = attend.astype(jnp.bfloat16)
    grad_attend = jnp.einsum(
        "thd,lhd->thl", grad_heads, value_heads, preferred_element_type=jnp.float32
    )
    row_dot = jnp.sum(attend * grad_attend, axis=2, keepdims=True)
    grad_scores = (attend * (grad_attend - row_dot) * factor).astype(jnp.bfloat16)
    grad_query = jnp.einsum(
        "thl,lhd->thd", grad_scores, key_heads, preferred_element_type=jnp.float32
    )
    grad_query = grad_query.astype(jnp.bfloat16).reshape(tokens_here, heads_here * HEAD_DIM)
    key_part = jnp.einsum(
        "thl,thd->lhd", grad_scores, query_heads, preferred_element_type=jnp.float32
    )
    value_part = jnp.einsum(
        "thl,thd->lhd", attend_half, grad_heads, preferred_element_type=jnp.float32
    )
    key_part = key_part.reshape(text_len, heads_here * HEAD_DIM)
    value_part = value_part.reshape(text_len, heads_here * HEAD_DIM)
    grad_keys, grad_values = sent_together((key_part, value_part), SEQ, 0, 1)
    grad_video = summed_on_arrival(
        lax.dot_general(
            grad_query, gathered, (((1,), (1,)), ((), ())), preferred_element_type=jnp.float32
        ).astype(jnp.bfloat16),
        "tp",
        0,
    )
    return (
        grad_video.astype(jnp.bfloat16),
        grad_keys.astype(jnp.bfloat16),
        grad_values.astype(jnp.bfloat16),
    )


def solution(mesh):
    split = Mesh(mesh.devices.reshape(4, 4, 4, mesh.shape["tp"]), ("seq_0", "seq_1", "seq_2", "tp"))
    in_specs = (P(SEQ, None), P(SEQ, "tp"), P(None, "tp"), P(None, "tp"), P(SEQ, "tp"))
    out_specs = (P(SEQ_TP, None), P(SEQ, "tp"), P(SEQ, "tp"))
    return jax.shard_map(local, mesh=split, in_specs=in_specs, out_specs=out_specs, check_vma=False)
```

profile of v0, /device:TPU:32, one launch (start us, length us, event | category | flops | bytes accessed | tf_op | source)
XLA Modules:
  0.0 265.8 jit_solution(12093132242676158325)
XLA Ops:
  7.2 0.0 all-gather.6.cloned.1.call-start
  7.3 19.3 %all-gather = bf16[320,640]{1,0:T(8,128)(2,1)} all-gather(bf16[80,640]{1,0:T(8,128)(2,1)} %param.6), channel_id=2, replica_groups=mesh['seq_0'=4,'seq_1'=4,'seq_2'=4,'tp'=8] {'seq_1'}, dimensions={0}, use_global_device_ids=true | all-gather | bytes 512000 | tf_op jit(solution)/shard_map/all_gather | solution.py:21
  26.6 0.0 all-gather.6.cloned.1.call-update
  26.6 0.0 all-gather.8.cloned.1.call-start
  26.6 35.1 %all-gather.6.cloned.1.call-done = bf16[16,80,640]{2,1,0:T(8,128)(2,1)} async-done(((bf16[4,80,640]{2,1,0:T(8,128)(2,1)}), bf16[16,80,640]{2,1,0:T(8,128)(2,1)}) %all-gather.6.cloned.1.call-update) | async-done | bytes 1638416 | tf_op jit(solution)/shard_map/all_gather | solution.py:21
  61.8 0.0 all-gather.8.cloned.1.call-update
  61.8 0.2 copy.46
  62.0 0.2 copy.50
  62.1 0.2 copy.49
  62.3 0.3 convolution_bitcast_fusion.2
  62.6 76.8 %all-gather.8.cloned.1.call-done = bf16[16,4,80,640]{3,2,1,0:T(8,128)(2,1)} async-done(((bf16[4,4,80,640]{3,2,1,0:T(8,128)(2,1)}), bf16[16,4,80,640]{3,2,1,0:T(8,128)(2,1)}) %all-gather.8.cloned.1.call-update) | async-done | bytes 6553616 | tf_op jit(solution)/shard_map/all_gather | solution.py:21
  139.3 3.7 %copy.44 = bf16[4,4,4,80,640]{4,3,2,1,0:T(8,128)(2,1)S(1)} copy(bf16[4,4,4,80,640]{4,3,1,0,2:T(8,128)(2,1)} %bitcast.47) | data formatting | bytes 13107200 | tf_op jit(solution)/shard_map/transpose | solution.py:24
  143.1 2.7 %copy-done.1 = bf16[4,4,4,80,640]{4,3,2,1,0:T(8,128)(2,1)} copy-done((bf16[4,4,4,80,640]{4,3,2,1,0:T(8,128)(2,1)}, bf16[4,4,4,80,640]{4,3,2,1,0:T(8,128)(2,1)S(1)}, u32[]{:S(2)}) %copy-start.1) | copy-done | bytes 6553624
  145.8 1.2 convolution_convert_fusion.2
  147.1 0.2 copy.45
  147.3 0.3 fusion.23
  147.6 0.5 convolution_bitcast_fusion
  148.0 1.0 convolution_bitcast_fusion.1
  149.1 1.2 copy.55
  150.3 0.2 concatenate.8
  150.5 0.2 copy.57
  150.7 0.2 concatenate.9
  150.9 1.2 pad_maximum_fusion
  152.1 10.1 %all-to-all-start.1 = ((f32[64,2,1280]{2,1,0:T(2,128)}), f32[64,2,1280]{2,1,0:T(2,128)S(1)}, u32[]{:S(2)}, u32[]{:S(2)}) async-start(f32[64,2,1280]{2,1,0:T(2,128)} %pad_maximum_fusion), calls=%async_computation.1 | async-start | bytes 1310720 | tf_op jit(solution)/shard_map/all_to_all | solution.py:39
  162.2 0.2 convolution_convert_fusion.1
  162.5 6.2 %convolution_convert_fusion = bf16[128,5120]{1,0:T(8,128)(2,1)} fusion(bf16[128,640]{0,1:T(8,128)(2,1)S(1)} %bitcast.60, bf16[5120,640]{1,0:T(8,128)(2,1)} %bitcast.46), kind=kOutput, calls=%fused_computation.2 | convolution fusion | flops 839516160 | bytes 8028160 | tf_op jit(solution)/shard_map/dot_general | solution.py:94
  168.6 11.9 %all-to-all-done.1 = f32[64,2,1280]{2,1,0:T(2,128)S(1)} async-done(((f32[64,2,1280]{2,1,0:T(2,128)}), f32[64,2,1280]{2,1,0:T(2,128)S(1)}, u32[]{:S(2)}, u32[]{:S(2)}) %all-to-all-start.1) | async-done | bytes 655392 | tf_op jit(solution)/shard_map/all_to_all | solution.py:39
  180.6 9.5 %all-to-all-start = ((bf16[8,16,5120]{2,1,0:T(8,128)(2,1)}), bf16[8,16,5120]{2,1,0:T(8,128)(2,1)S(1)}, u32[]{:S(2)}, u32[]{:S(2)}) async-start(bf16[8,16,5120]{2,1,0:T(8,128)(2,1)} %bitcast.48), calls=%async_computation | async-start | bytes 2621440 | tf_op jit(solution)/shard_map/all_to_all | solution.py:52
  190.0 0.2 reduce_sum.42
  190.3 0.6 fusion.22
  190.9 67.3 %all-to-all-done = bf16[8,16,5120]{2,1,0:T(8,128)(2,1)S(1)} async-done(((bf16[8,16,5120]{2,1,0:T(8,128)(2,1)}), bf16[8,16,5120]{2,1,0:T(8,128)(2,1)S(1)}, u32[]{:S(2)}, u32[]{:S(2)}) %all-to-all-start) | async-done | bytes 1310752 | tf_op jit(solution)/shard_map/all_to_all | solution.py:52
  258.1 0.9 reduce_sum.41
  (9 shorter events, 0.0 us)
Async XLA Ops:
  7.2 138.7 %copy-start = (bf16[128,5120]{1,0:T(8,128)(2,1)S(1)}, bf16[128,5120]{1,0:T(8,128)(2,1)}, u32[]{:S(2)}) copy-start(bf16[128,5120]{1,0:T(8,128)(2,1)} %param.5) | copy-start | bytes 3932164
  7.2 54.6 %copy-start.2 = (bf16[128,640]{1,0:T(8,128)(2,1)S(1)}, bf16[128,640]{1,0:T(8,128)(2,1)}, u32[]{:S(2)}) copy-start(bf16[128,640]{1,0:T(8,128)(2,1)} %param.7) | copy-start | bytes 491524
  7.2 54.8 %copy-start.3 = (bf16[128,640]{1,0:T(8,128)(2,1)S(1)}, bf16[128,640]{1,0:T(8,128)(2,1)}, u32[]{:S(2)}) copy-start(bf16[128,640]{1,0:T(8,128)(2,1)} %param.9) | copy-start | bytes 491524
  7.2 54.9 %copy-start.4 = (bf16[128,640]{1,0:T(8,128)(2,1)S(1)}, bf16[128,640]{1,0:T(8,128)(2,1)}, u32[]{:S(2)}) copy-start(bf16[128,640]{1,0:T(8,128)(2,1)} %param.8) | copy-start | bytes 491524
  7.2 54.5 %all-gather.6.cloned.1.call-start = ((), (), s32[]{:S(2)}) async-start(), calls=%async_computation.2 | async-start | bytes 2048000 | tf_op jit(solution)/shard_map/all_gather | solution.py:21
  26.6 112.8 %all-gather.8.cloned.1.call-start = ((), (), s32[]{:S(2)}) async-start(), calls=%async_computation.3 | async-start | bytes 8192000 | tf_op jit(solution)/shard_map/all_gather | solution.py:21
  143.1 2.7 %copy-start.1 = (bf16[4,4,4,80,640]{4,3,2,1,0:T(8,128)(2,1)}, bf16[4,4,4,80,640]{4,3,2,1,0:T(8,128)(2,1)S(1)}, u32[]{:S(2)}) copy-start(bf16[4,4,4,80,640]{4,3,2,1,0:T(8,128)(2,1)S(1)} %copy.44) | copy-start | bytes 19660804
  152.1 28.5 %all-to-all-start.1 = ((f32[64,2,1280]{2,1,0:T(2,128)}), f32[64,2,1280]{2,1,0:T(2,128)S(1)}, u32[]{:S(2)}, u32[]{:S(2)}) async-start(f32[64,2,1280]{2,1,0:T(2,128)} %pad_maximum_fusion), calls=%async_computation.1 | async-start | bytes 1310720 | tf_op jit(solution)/shard_map/all_to_all | solution.py:39
  180.6 77.6 %all-to-all-start = ((bf16[8,16,5120]{2,1,0:T(8,128)(2,1)}), bf16[8,16,5120]{2,1,0:T(8,128)(2,1)S(1)}, u32[]{:S(2)}, u32[]{:S(2)}) async-start(bf16[8,16,5120]{2,1,0:T(8,128)(2,1)} %bitcast.48), calls=%async_computation | async-start | bytes 2621440 | tf_op jit(solution)/shard_map/all_to_all | solution.py:52
Sparse Core Ops, SparseCore 0:
  26.7 35.0 all-gather.5
  63.9 75.4 all-gather.7
where the time goes:
time: 266 us
  waiting for transfers between devices  191 us (72%)
  starting transfers between devices  19.7 us (7%)
  blocking collectives  19.3 us (7%)
  between operations  14.2 us (5%)
  matrix products  9.72 us (4%)
  local copies, waits for them, and re-layouts  9.57 us (4%)
    all_gather x2, waiting for transfers between devices, all_blocks(): tiles = lax.all_gather(tiles, axes[k])  112 us
    all_to_all x1, waiting for transfers between devices, summed_on_arrival(): tiles = lax.all_to_all(split_up(x, dim, length), axis, 0, 0, tiled=True)  67.3 us
    all_gather x1, blocking collectives, all_blocks(): tiles = lax.all_gather(tiles, axes[k])  19.3 us
    all_to_all x1, waiting for transfers between devices, sum_at_owner(): tiles = lax.all_to_all(split_up(x, dim, length), axis, 0, 0, tiled=True)  11.9 us
    all_to_all x1, starting transfers between devices, sum_at_owner(): tiles = lax.all_to_all(split_up(x, dim, length), axis, 0, 0, tiled=True)  10.1 us
    all_to_all x1, starting transfers between devices, summed_on_arrival(): tiles = lax.all_to_all(split_up(x, dim, length), axis, 0, 0, tiled=True)  9.48 us
    dot_general x1, matrix products, local(): lax.dot_general(grad_query, gathered, (((1,), (1,)), ((), ())), preferred...  6.17 us
  transfers between devices with their start and end apart: 4, of which 4 were waited for; matrix products, arithmetic and copies ran while one was open for 3% of the time, Pallas kernels for 0%

commit v1 on v0

v1 whole, which is shorter than its diff:
```python
import jax
import jax.numpy as jnp
from jax import lax
from jax.experimental import pallas as pl
from jax.experimental.pallas import tpu as pltpu
from jax.sharding import Mesh
from jax.sharding import PartitionSpec as P

HEAD_DIM = 128
HEADS = 5
ROWS = 80
TOKENS = 128
TEXT = 128
DEPTH = 5120
CHUNK = 1280
WIDTH = HEADS * HEAD_DIM
AXES = ("y", "zl", "x", "zh", "c")
SEQ = ("y", "zl", "x")
COPIES = 87
F32 = jnp.float32
BF16 = jnp.bfloat16


def dot(a, b, dims):
    return lax.dot_general(a, b, ((dims[:1], dims[1:]), ((), ())), preferred_element_type=F32)


class Mail:
    def __init__(self, send_sems, recv_sems):
        self.send_sems, self.recv_sems, self.sent = send_sems, recv_sems, []

    def send(self, src, dst, **where):
        at = len(self.sent)
        copy = pltpu.make_async_remote_copy(
            src_ref=src,
            dst_ref=dst,
            send_sem=self.send_sems.at[at],
            recv_sem=self.recv_sems.at[at],
            device_id=where,
            device_id_type=pl.DeviceIdType.MESH,
        )
        copy.start()
        self.sent.append(copy)
        return copy

    def same(self, ref, **where):
        return self.send(ref, ref, **where)


def arrived(*copies):
    for copy in copies:
        copy.wait_recv()


def kernel(
    video_hbm, weight_hbm, keys_hbm, values_hbm, grad_hbm,
    out_video, out_keys, out_values,
    video, keys_in, values_in, grad, keys, weight, grad_att, grad_query,
    kv, kv_x, kv_y, kv_mid, kv_z_src, kv_z,
    part, part_in, total, far, relay, near_up, near_down,
    local_sems, send_sems, recv_sems,
):
    y, z, x = lax.axis_index("y"), lax.axis_index("zl"), lax.axis_index("x")
    h, c = lax.axis_index("zh"), lax.axis_index("c")
    yn, yp, xn, xp = (y + 3) % 4, (y + 1) % 4, (x + 3) % 4, (x + 1) % 4
    hn, hp, hf = (h + 3) % 4, (h + 1) % 4, (h + 2) % 4
    z_others = (z + 1 - 2 * (z % 2), (z + 2) % 4, 3 - z)
    near = 2 * (z // 2)
    other = 2 - near
    factor = HEAD_DIM ** (-0.5)

    own = [
        pltpu.make_async_copy(
            weight_hbm.at[:, pl.ds(k * HEAD_DIM, HEAD_DIM)], weight.at[k, y, z, x], local_sems.at[k]
        )
        for k in range(HEADS)
    ]
    loads = [
        pltpu.make_async_copy(src, dst, local_sems.at[HEADS + k])
        for k, (src, dst) in enumerate(
            ((keys_hbm, keys_in), (values_hbm, values_in), (grad_hbm, grad), (video_hbm, video))
        )
    ]
    for copy in own + loads:
        copy.start()

    barrier = pltpu.get_barrier_semaphore()
    partners = (
        [{"zl": k} for k in z_others]
        + [{"x": k} for k in (xp, xn, (x + 2) % 4)]
        + [{"y": k} for k in (yp, yn, (y + 2) % 4)]
        + [{"zh": hp}, {"zh": hn}, {"c": 1 - c}]
    )
    for where in partners:
        pl.semaphore_signal(barrier, inc=1, device_id=where, device_id_type=pl.DeviceIdType.MESH)
    pl.semaphore_wait(barrier, len(partners))
    for copy in own:
        copy.wait()

    mail = Mail(send_sems, recv_sems)
    near_pair, other_pair = pl.ds(near, 2), pl.ds(other, 2)

    def z_step(g):
        return [mail.same(weight.at[g, y, z, x], zl=k) for k in z_others]

    def small_y(g):
        ref = weight.at[g, y, near_pair, x]
        return mail.same(ref, y=yp), mail.same(ref, y=yn)

    def small_x(g):
        ref = weight.at[g, y, other_pair, x]
        return mail.same(ref, x=xp), mail.same(ref, x=xn)

    def small_y_on(g):
        return (
            mail.same(weight.at[g, yn, near, x], y=yp),
            mail.same(weight.at[g, yp, near + 1, x], y=yn),
        )

    def small_x_on(g):
        return (
            mail.same(weight.at[g, y, other, xn], x=xp),
            mail.same(weight.at[g, y, other + 1, xp], x=xn),
        )

    def big_x(k):
        ref = weight.at[k, :, near_pair, x]
        return mail.same(ref, x=xp), mail.same(ref, x=xn)

    def big_y(k):
        ref = weight.at[k, y, other_pair]
        return mail.same(ref, y=yp), mail.same(ref, y=yn)

    def big_on(k):
        return (
            mail.same(weight.at[k, :, near, xn], x=xp),
            mail.same(weight.at[k, :, near + 1, xp], x=xn),
            mail.same(weight.at[k, yn, other], y=yp),
            mail.same(weight.at[k, yp, other + 1], y=yn),
        )

    first, rest = pl.ds(0, 1), pl.ds(1, HEADS - 1)
    z0 = z_step(first)
    z1 = z_step(rest)

    def columns(k):
        return slice(k * HEAD_DIM, (k + 1) * HEAD_DIM)

    for copy in loads[:3]:
        copy.wait()
    row = lax.broadcasted_iota(jnp.int32, (TEXT, TEXT), 0)
    col = lax.broadcasted_iota(jnp.int32, (TEXT, TEXT), 1)
    source = (row // 8 % 4) * 32 + (row // 2 % 4) * 8 + (row // 32) * 2 + row % 2
    pick = jnp.where(col == source, 1.0, 0.0).astype(BF16)
    keys[...] = dot(pick, keys_in[...], (1, 0)).astype(BF16)
    for k in range(HEADS):
        values_k = dot(pick, values_in[:, columns(k)], (1, 0)).astype(BF16)
        grad_att[k] = dot(values_k, grad[:, columns(k)], (1, 1))
    loads[3].wait()

    def attention(k):
        query = jnp.zeros((TOKENS, HEAD_DIM), F32)
        for j in range(4):
            query += dot(
                video[:, j * CHUNK : (j + 1) * CHUNK], weight[k, j].reshape(CHUNK, HEAD_DIM), (1, 0)
            )
        query = query.astype(BF16)
        keys_k = keys[:, columns(k)]
        scores = dot(keys_k, query, (1, 1)) * factor
        raised = jnp.exp(scores - jnp.max(scores, axis=0, keepdims=True))
        attend = raised / jnp.sum(raised, axis=0, keepdims=True)
        grad_attend = grad_att[k]
        row_dot = jnp.sum(attend * grad_attend, axis=0, keepdims=True)
        grad_scores = (attend * (grad_attend - row_dot) * factor).astype(BF16)
        grad_query[:, columns(k)] = dot(grad_scores, keys_k, (0, 0)).astype(BF16)
        key_part = dot(grad_scores, query, (1, 0))
        value_part = dot(attend.astype(BF16), grad[:, columns(k)], (1, 0))
        kv[0, :, :, columns(k)] = key_part.reshape(4, 32, HEAD_DIM)
        kv[1, :, :, columns(k)] = value_part.reshape(4, 32, HEAD_DIM)

    arrived(z0[0])
    y0 = small_y(first)
    arrived(*z0[1:])
    x0 = small_x(first)
    arrived(*y0)
    y0_on = small_y_on(first)
    arrived(*x0)
    x0_on = small_x_on(first)
    arrived(z1[0])
    y1 = small_y(rest)
    arrived(*z1[1:])
    x1 = small_x(rest)
    arrived(*y0_on)
    big = {}
    big[0] = big_x(0)
    arrived(*x0_on)
    big[0] += big_y(0)
    arrived(*y1)
    y1_on = small_y_on(rest)
    arrived(*x1)
    x1_on = small_x_on(rest)
    arrived(*y1_on)
    big[1] = big_x(1)
    arrived(*x1_on)
    big[1] += big_y(1)
    big_done = {}
    for k in range(HEADS):
        arrived(*big[k])
        big_done[k] = big_on(k)
        if k + 2 < HEADS:
            big[k + 2] = big_x(k + 2) + big_y(k + 2)
        if k >= 1:
            arrived(*big_done[k - 1])
            attention(k - 1)
    arrived(*big_done[HEADS - 1])
    attention(HEADS - 1)

    x_far, y_far = (x + 2) % 4, (y + 2) % 4
    kv_x_in = [
        mail.send(kv.at[:, to], kv_x.at[n], x=to) for n, to in enumerate((xp, xn, x_far))
    ]

    order = (0, 2, 1, 3)
    pair_in = {}
    for j in order:
        made = jnp.zeros((TOKENS, CHUNK), F32)
        for k in range(HEADS):
            made += dot(grad_query[:, columns(k)], weight[k, j].reshape(CHUNK, HEAD_DIM), (1, 1))
        made = made.astype(BF16)
        for t in range(8):
            part[j, t % 2, t // 2] = made[t * 16 : (t + 1) * 16]
        pair_in[j] = mail.send(part.at[j, 1 - c], part_in.at[j], c=1 - c)
    far_in, up_in, down_in = {}, {}, {}
    for j in order:
        arrived(pair_in[j])
        total[j] = (part[j, c].astype(F32) + part_in[j].astype(F32)).astype(BF16)
        if j < 2:
            far_in[j] = mail.send(total.at[j, hf], far.at[j], zh=hp)
            down_in[j] = mail.send(total.at[j, hn], near_down.at[j], zh=hn)
        else:
            far_in[j] = mail.send(total.at[j, hf], far.at[j], zh=hn)
            up_in[j] = mail.send(total.at[j, hp], near_up.at[j], zh=hp)
    for j in order:
        arrived(far_in[j])
        to = hp if j < 2 else hn
        relay[j] = (total[j, to].astype(F32) + far[j].astype(F32)).astype(BF16)
        if j < 2:
            up_in[j] = mail.send(relay.at[j], near_up.at[j], zh=hp)
        else:
            down_in[j] = mail.send(relay.at[j], near_down.at[j], zh=hn)

    arrived(*kv_x_in)
    kv_mid[...] = (kv[:, x] + kv_x[0] + kv_x[1] + kv_x[2]).reshape(2, 4, 8, WIDTH)
    kv_y_in = [
        mail.send(kv_mid.at[:, to], kv_y.at[n], y=to) for n, to in enumerate((yp, yn, y_far))
    ]
    arrived(*kv_y_in)
    mine = kv_mid[:, y] + kv_y[0] + kv_y[1] + kv_y[2]
    for j in range(4):
        kv_z_src[j] = mine[:, 2 * j : 2 * j + 2]
    kv_z_in = [
        mail.send(kv_z_src.at[to], kv_z.at[n], zl=to) for n, to in enumerate(z_others)
    ]

    for j in order:
        arrived(up_in[j], down_in[j])
        out_video[:, j * CHUNK : (j + 1) * CHUNK] = (
            total[j, h].astype(F32) + near_up[j].astype(F32) + near_down[j].astype(F32)
        ).astype(BF16)
    arrived(*kv_z_in)
    both = kv_z_src[z] + kv_z[0] + kv_z[1] + kv_z[2]
    out_keys[...] = both[0].astype(BF16)
    out_values[...] = both[1].astype(BF16)
    assert len(mail.sent) == COPIES, len(mail.sent)
    for copy in mail.sent:
        copy.wait_send()


def local(video_tokens, w_query, text_keys, text_values, grad_out):
    vmem = pltpu.VMEM
    return pl.pallas_call(
        kernel,
        out_shape=(
            jax.ShapeDtypeStruct((16, DEPTH), BF16),
            jax.ShapeDtypeStruct((2, WIDTH), BF16),
            jax.ShapeDtypeStruct((2, WIDTH), BF16),
        ),
        in_specs=[pl.BlockSpec(memory_space=pl.ANY)] * 5,
        out_specs=(pl.BlockSpec(memory_space=pltpu.VMEM),) * 3,
        scratch_shapes=[
            vmem((TOKENS, DEPTH), BF16),
            vmem((TEXT, WIDTH), BF16),
            vmem((TEXT, WIDTH), BF16),
            vmem((TOKENS, WIDTH), BF16),
            vmem((TEXT, WIDTH), BF16),
            vmem((HEADS, 4, 4, 4, ROWS, HEAD_DIM), BF16),
            vmem((HEADS, TEXT, TOKENS), F32),
            vmem((TOKENS, WIDTH), BF16),
            vmem((2, 4, 32, WIDTH), F32),
            vmem((3, 2, 32, WIDTH), F32),
            vmem((3, 2, 8, WIDTH), F32),
            vmem((2, 4, 8, WIDTH), F32),
            vmem((4, 2, 2, WIDTH), F32),
            vmem((3, 2, 2, WIDTH), F32),
            vmem((4, 2, 4, 16, CHUNK), BF16),
            vmem((4, 4, 16, CHUNK), BF16),
            vmem((4, 4, 16, CHUNK), BF16),
            vmem((4, 16, CHUNK), BF16),
            vmem((4, 16, CHUNK), BF16),
            vmem((4, 16, CHUNK), BF16),
            vmem((4, 16, CHUNK), BF16),
            pltpu.SemaphoreType.DMA((HEADS + 4,)),
            pltpu.SemaphoreType.DMA((COPIES,)),
            pltpu.SemaphoreType.DMA((COPIES,)),
        ],
        compiler_params=pltpu.CompilerParams(collective_id=0, has_side_effects=True),
    )(video_tokens, w_query, text_keys, text_values, grad_out)


def solution(mesh):
    split = Mesh(mesh.devices.reshape(4, 4, 4, 4, 2), AXES)
    tp = ("zh", "c")
    in_specs = (P(SEQ, None), P(SEQ, tp), P(None, tp), P(None, tp), P(SEQ, tp))
    out_specs = (P(AXES, None), P(SEQ, tp), P(SEQ, tp))
    return jax.shard_map(local, mesh=split, in_specs=in_specs, out_specs=out_specs, check_vma=False)
```

time: 266 us -> 99.6 us (0.37)
  the two profiles are of different devices: /device:TPU:32 before, /device:TPU:1 now
where the time goes in v1:
time: 99.6 us; the launch traced here: 99.4 us
  Pallas kernels  94.6 us (95%)
  local copies, waits for them, and re-layouts  4.1 us (4%)
    pallas_call x1, Pallas kernels, local(): pl.pallas_call(kernel, out_shape=(jax.ShapeDtypeStruct((16, DEPTH), BF16)...  94.6 us
    unnamed x3, local copies, waits for them, and re-layouts  4.1 us

profile of v1, /device:TPU:1, one launch (start us, length us, event | category | flops | bytes accessed | tf_op | source)
XLA Modules:
  0.0 99.4 jit_solution(1252283000244489809)
XLA Ops:
  0.6 94.6 %shard_map.76 = (bf16[16,5120]{1,0:T(8,128)(2,1)}, bf16[2,640]{1,0:T(2,128)(2,1)}, bf16[2,640]{1,0:T(2,128)(2,1)}) custom-call(bf16[128,5120]{1,0:T(8,128)(2,1)} %video_hbm.1, bf16[80,640]{1,0:T(8,128)(2,1)} %weight_hbm.1, bf16[128,640]{1,0:T(8,128)(2,1)} %keys_hbm.1, bf16[128,640]{1,0:T(8,128)(2,1)} %values_hbm.1, bf16[128,640]{1,0:T(8,128)(2,1)} %grad_hbm.1), custom_call_target="tpu_custom_call" | custom-call | tf_op jit(solution)/shard_map/pallas_call | solution.py:281
  95.3 1.6 %copy.11 = bf16[16,5120]{1,0:T(8,128)(2,1)} copy(bf16[16,5120]{1,0:T(8,128)(2,1)} %get-tuple-element.6) | data formatting | bytes 327680
  96.9 1.3 %copy.12 = bf16[2,640]{1,0:T(2,128)(2,1)} copy(bf16[2,640]{1,0:T(2,128)(2,1)} %get-tuple-element.7) | data formatting | bytes 5120
  98.1 1.2 %copy.13 = bf16[2,640]{1,0:T(2,128)(2,1)} copy(bf16[2,640]{1,0:T(2,128)(2,1)} %get-tuple-element.8) | data formatting | bytes 5120

commit v2 on v1

--- a/solution.py
+++ b/solution.py
@@ -16,7 +16,7 @@
 WIDTH = HEADS * HEAD_DIM
 AXES = ("y", "zl", "x", "zh", "c")
 SEQ = ("y", "zl", "x")
-COPIES = 87
+COPIES = 126
 F32 = jnp.float32
 BF16 = jnp.bfloat16
 
@@ -27,10 +27,11 @@
 
 class Mail:
     def __init__(self, send_sems, recv_sems):
-        self.send_sems, self.recv_sems, self.sent = send_sems, recv_sems, []
-
-    def send(self, src, dst, **where):
-        at = len(self.sent)
+        self.send_sems, self.recv_sems = send_sems, recv_sems
+        self.made, self.sent = [], []
+
+    def make(self, src, dst, **where):
+        at = len(self.made)
         copy = pltpu.make_async_remote_copy(
             src_ref=src,
             dst_ref=dst,
@@ -39,6 +40,11 @@
             device_id=where,
             device_id_type=pl.DeviceIdType.MESH,
         )
+        self.made.append(copy)
+        return copy
+
+    def send(self, src, dst, **where):
+        copy = self.make(src, dst, **where)
         copy.start()
         self.sent.append(copy)
         return copy
@@ -55,13 +61,14 @@
 def kernel(
     video_hbm, weight_hbm, keys_hbm, values_hbm, grad_hbm,
     out_video, out_keys, out_values,
-    video, keys_in, values_in, grad, keys, weight, grad_att, grad_query,
-    kv, kv_x, kv_y, kv_mid, kv_z_src, kv_z,
+    video, keys_in, values_in, grad, keys, weight, grad_att, grad_query, made,
+    kv, kv_1, kv_2, kv_mid, kv_z_src, kv_z,
     part, part_in, total, far, relay, near_up, near_down,
     local_sems, send_sems, recv_sems,
 ):
     y, z, x = lax.axis_index("y"), lax.axis_index("zl"), lax.axis_index("x")
     h, c = lax.axis_index("zh"), lax.axis_index("c")
+    yf, xf = (y + 2) % 4, (x + 2) % 4
     yn, yp, xn, xp = (y + 3) % 4, (y + 1) % 4, (x + 3) % 4, (x + 1) % 4
     hn, hp, hf = (h + 3) % 4, (h + 1) % 4, (h + 2) % 4
     z_others = (z + 1 - 2 * (z % 2), (z + 2) % 4, 3 - z)
@@ -139,9 +146,21 @@
             mail.same(weight.at[k, yp, other + 1], y=yn),
         )
 
-    first, rest = pl.ds(0, 1), pl.ds(1, HEADS - 1)
-    z0 = z_step(first)
-    z1 = z_step(rest)
+    last = HEADS - 1
+    rows_a, rows_b = pl.ds(0, 40), pl.ds(40, 40)
+    single, double = (lambda k: pl.ds(k, 1)), pl.ds(2, 2)
+    z0 = z_step(single(0))
+    a_ref, b_ref = weight.at[last, y, z, x, rows_a], weight.at[last, y, z, x, rows_b]
+    a1 = [mail.same(a_ref, x=to) for to in (xp, xn, (x + 2) % 4)]
+    b1 = [mail.same(b_ref, y=to) for to in (yp, yn, (y + 2) % 4)]
+    z1 = z_step(single(1))
+    z2 = z_step(double)
+
+    def by_x(ref):
+        return mail.same(ref, x=xp), mail.same(ref, x=xn)
+
+    def by_y(ref):
+        return mail.same(ref, y=yp), mail.same(ref, y=yn)
 
     def columns(k):
         return slice(k * HEAD_DIM, (k + 1) * HEAD_DIM)
@@ -153,10 +172,12 @@
     source = (row // 8 % 4) * 32 + (row // 2 % 4) * 8 + (row // 32) * 2 + row % 2
     pick = jnp.where(col == source, 1.0, 0.0).astype(BF16)
     keys[...] = dot(pick, keys_in[...], (1, 0)).astype(BF16)
-    for k in range(HEADS):
-        values_k = dot(pick, values_in[:, columns(k)], (1, 0)).astype(BF16)
-        grad_att[k] = dot(values_k, grad[:, columns(k)], (1, 1))
     loads[3].wait()
+
+    def prepare():
+        for k in range(HEADS):
+            values_k = dot(pick, values_in[:, columns(k)], (1, 0)).astype(BF16)
+            grad_att[k] = dot(values_k, grad[:, columns(k)], (1, 1))
 
     def attention(k):
         query = jnp.zeros((TOKENS, HEAD_DIM), F32)
@@ -175,72 +196,144 @@
         grad_query[:, columns(k)] = dot(grad_scores, keys_k, (0, 0)).astype(BF16)
         key_part = dot(grad_scores, query, (1, 0))
         value_part = dot(attend.astype(BF16), grad[:, columns(k)], (1, 0))
-        kv[0, :, :, columns(k)] = key_part.reshape(4, 32, HEAD_DIM)
-        kv[1, :, :, columns(k)] = value_part.reshape(4, 32, HEAD_DIM)
-
+        kv[0, :, :, :, columns(k)] = key_part.reshape(4, 4, 8, HEAD_DIM)
+        kv[1, :, :, :, columns(k)] = value_part.reshape(4, 4, 8, HEAD_DIM)
+
+    def back(k, j):
+        return dot(grad_query[:, columns(k)], weight[k, j].reshape(CHUNK, HEAD_DIM), (1, 1))
+
+    def gather_back(k):
+        for j in range(4):
+            made[j] = back(k, j) if k == 0 else made[j] + back(k, j)
+
+    def small_a():
+        ref = weight.at[last, y, z, :, rows_a]
+        return mail.same(ref, y=yp), mail.same(ref, y=yn)
+
+    def small_b():
+        ref = weight.at[last, :, z, x, rows_b]
+        return mail.same(ref, x=xp), mail.same(ref, x=xn)
+
+    sent_if = []
+
+    def plane_send(which, go, to):
+        ref = weight.at[last, :, which]
+        copy = mail.make(ref, ref, zl=to)
+        pl.when(go)(copy.start)
+        sent_if.append((copy, go))
+        return copy
+
+    def plane_arrived(copy, go):
+        pl.when(go)(copy.wait_recv)
+
+    z_up, z_down = (z + 1) % 4, (z + 3) % 4
+
+    def planes(step):
+        lower, upper = (z + 4 - step) % 4, (z + step) % 4
+        up = plane_send(lower, jnp.logical_and(z >= step, z < 3), z_up)
+        down = plane_send(upper, jnp.logical_and(z + step <= 3, z > 0), z_down)
+        return up, down
+
+    def planes_in(copies, step):
+        plane_arrived(copies[0], z >= step + 1)
+        plane_arrived(copies[1], z + step + 1 <= 3)
+
+    prepare()
     arrived(z0[0])
-    y0 = small_y(first)
+    y0 = small_y(single(0))
+    slices = by_x(weight.at[0, y, near_pair, x])
     arrived(*z0[1:])
-    x0 = small_x(first)
+    x0 = small_x(single(0))
+    slices += by_y(weight.at[0, y, other_pair, x])
+    arrived(*a1)
+    a2 = small_a()
+    arrived(*b1)
+    b2 = small_b()
     arrived(*y0)
-    y0_on = small_y_on(first)
+    y0_on = small_y_on(single(0))
+    slices += by_x(weight.at[0, yn, near_pair, x]) + by_x(weight.at[0, yp, near_pair, x])
+    arrived(z1[0])
+    y1 = small_y(single(1))
     arrived(*x0)
-    x0_on = small_x_on(first)
-    arrived(z1[0])
-    y1 = small_y(rest)
+    x0_on = small_x_on(single(0))
+    slices += by_y(weight.at[0, y, other_pair, xn]) + by_y(weight.at[0, y, other_pair, xp])
     arrived(*z1[1:])
-    x1 = small_x(rest)
+    x1 = small_x(single(1))
     arrived(*y0_on)
-    big = {}
-    big[0] = big_x(0)
+    slices += by_x(weight.at[0, yf, near_pair, x])
+    arrived(*a2)
+    a2_on = mail.same(weight.at[last, yn, z, :, rows_a], y=yp)
+    arrived(*b2)
+    b2_on = mail.same(weight.at[last, :, z, xn, rows_b], x=xp)
     arrived(*x0_on)
-    big[0] += big_y(0)
+    slices += by_y(weight.at[0, y, other_pair, xf])
+    big, big_done, plane = {}, {}, {}
     arrived(*y1)
-    y1_on = small_y_on(rest)
+    y1_on = small_y_on(single(1))
     arrived(*x1)
-    x1_on = small_x_on(rest)
+    x1_on = small_x_on(single(1))
+    arrived(z2[0])
+    y2 = small_y(double)
+    arrived(*z2[1:])
+    x2 = small_x(double)
+    arrived(a2_on, b2_on)
+    plane[0] = planes(0)
     arrived(*y1_on)
     big[1] = big_x(1)
     arrived(*x1_on)
     big[1] += big_y(1)
-    big_done = {}
-    for k in range(HEADS):
-        arrived(*big[k])
-        big_done[k] = big_on(k)
-        if k + 2 < HEADS:
-            big[k + 2] = big_x(k + 2) + big_y(k + 2)
-        if k >= 1:
-            arrived(*big_done[k - 1])
-            attention(k - 1)
-    arrived(*big_done[HEADS - 1])
-    attention(HEADS - 1)
-
-    x_far, y_far = (x + 2) % 4, (y + 2) % 4
-    kv_x_in = [
-        mail.send(kv.at[:, to], kv_x.at[n], x=to) for n, to in enumerate((xp, xn, x_far))
-    ]
+    arrived(*y2)
+    y2_on = small_y_on(double)
+    arrived(*x2)
+    x2_on = small_x_on(double)
+    arrived(*slices)
+    big_done[0] = big_on(0)
+    arrived(*y2_on, *x2_on)
+    big[2] = big_x(2) + big_y(2)
+    arrived(*big[1])
+    big_done[1] = big_on(1)
+    big[3] = big_x(3) + big_y(3)
+    planes_in(plane[0], 0)
+    plane[1] = planes(1)
+    arrived(*big_done[0])
+    attention(0)
+    gather_back(0)
+    arrived(*big[2])
+    big_done[2] = big_on(2)
+    arrived(*big_done[1])
+    attention(1)
+    gather_back(1)
+    planes_in(plane[1], 1)
+    plane[2] = planes(2)
+    arrived(*big[3])
+    big_done[3] = big_on(3)
+    arrived(*big_done[2])
+    attention(2)
+    gather_back(2)
+    arrived(*big_done[3])
+    planes_in(plane[2], 2)
+    attention(3)
+    attention(4)
+
+    key_in = [mail.send(kv.at[0, to], kv_1.at[0, n], x=to) for n, to in enumerate((xp, xn, xf))]
+    value_in = [mail.send(kv.at[1, :, to], kv_1.at[1, n], y=to) for n, to in enumerate((yp, yn, yf))]
 
     order = (0, 2, 1, 3)
-    pair_in = {}
-    for j in order:
-        made = jnp.zeros((TOKENS, CHUNK), F32)
-        for k in range(HEADS):
-            made += dot(grad_query[:, columns(k)], weight[k, j].reshape(CHUNK, HEAD_DIM), (1, 1))
-        made = made.astype(BF16)
+    pair_in, far_in, up_in, down_in = {}, {}, {}, {}
+
+    def make_part(j):
+        whole = (made[j] + back(3, j) + back(4, j)).astype(BF16)
         for t in range(8):
-            part[j, t % 2, t // 2] = made[t * 16 : (t + 1) * 16]
+            part[j, t % 2, t // 2] = whole[t * 16 : (t + 1) * 16]
         pair_in[j] = mail.send(part.at[j, 1 - c], part_in.at[j], c=1 - c)
-    far_in, up_in, down_in = {}, {}, {}
-    for j in order:
+
+    def make_total(j):
         arrived(pair_in[j])
         total[j] = (part[j, c].astype(F32) + part_in[j].astype(F32)).astype(BF16)
-        if j < 2:
-            far_in[j] = mail.send(total.at[j, hf], far.at[j], zh=hp)
-            down_in[j] = mail.send(total.at[j, hn], near_down.at[j], zh=hn)
-        else:
-            far_in[j] = mail.send(total.at[j, hf], far.at[j], zh=hn)
-            up_in[j] = mail.send(total.at[j, hp], near_up.at[j], zh=hp)
-    for j in order:
+        to = hp if j < 2 else hn
+        far_in[j] = mail.send(total.at[j, hf], far.at[j], zh=to)
+
+    def send_on(j):
         arrived(far_in[j])
         to = hp if j < 2 else hn
         relay[j] = (total[j, to].astype(F32) + far[j].astype(F32)).astype(BF16)
@@ -249,18 +342,34 @@
         else:
             down_in[j] = mail.send(relay.at[j], near_down.at[j], zh=hn)
 
-    arrived(*kv_x_in)
-    kv_mid[...] = (kv[:, x] + kv_x[0] + kv_x[1] + kv_x[2]).reshape(2, 4, 8, WIDTH)
-    kv_y_in = [
-        mail.send(kv_mid.at[:, to], kv_y.at[n], y=to) for n, to in enumerate((yp, yn, y_far))
-    ]
-    arrived(*kv_y_in)
-    mine = kv_mid[:, y] + kv_y[0] + kv_y[1] + kv_y[2]
-    for j in range(4):
-        kv_z_src[j] = mine[:, 2 * j : 2 * j + 2]
-    kv_z_in = [
-        mail.send(kv_z_src.at[to], kv_z.at[n], zl=to) for n, to in enumerate(z_others)
-    ]
+    make_part(0)
+    make_part(2)
+    make_part(1)
+    make_total(0)
+    make_part(3)
+    make_total(2)
+    make_total(1)
+    make_total(3)
+    for j in (0, 1):
+        down_in[j] = mail.send(total.at[j, hn], near_down.at[j], zh=hn)
+        up_in[j + 2] = mail.send(total.at[j + 2, hp], near_up.at[j + 2], zh=hp)
+
+    arrived(*key_in)
+    kv_mid[0] = kv[0, x] + kv_1[0, 0] + kv_1[0, 1] + kv_1[0, 2]
+    key_in = [mail.send(kv_mid.at[0, to], kv_2.at[0, n], y=to) for n, to in enumerate((yp, yn, yf))]
+    arrived(*value_in)
+    kv_mid[1] = kv[1, :, y] + kv_1[1, 0] + kv_1[1, 1] + kv_1[1, 2]
+    value_in = [mail.send(kv_mid.at[1, to], kv_2.at[1, n], x=to) for n, to in enumerate((xp, xn, xf))]
+    send_on(0)
+    send_on(2)
+    arrived(*key_in, *value_in)
+    for k, at in enumerate((y, x)):
+        rows = kv_mid[k, at] + kv_2[k, 0] + kv_2[k, 1] + kv_2[k, 2]
+        for j in range(4):
+            kv_z_src[j, k] = rows[2 * j : 2 * j + 2]
+    kv_z_in = [mail.send(kv_z_src.at[to], kv_z.at[n], zl=to) for n, to in enumerate(z_others)]
+    send_on(1)
+    send_on(3)
 
     for j in order:
         arrived(up_in[j], down_in[j])
@@ -271,20 +380,29 @@
     both = kv_z_src[z] + kv_z[0] + kv_z[1] + kv_z[2]
     out_keys[...] = both[0].astype(BF16)
     out_values[...] = both[1].astype(BF16)
-    assert len(mail.sent) == COPIES, len(mail.sent)
+    assert len(mail.made) == COPIES, len(mail.made)
     for copy in mail.sent:
         copy.wait_send()
+    for copy, go in sent_if:
+        pl.when(go)(copy.wait_send)
+
+
+def hand_over(a_in, b_in, c_in, a_out, b_out, c_out):
+    a_out[...] = a_in[...]
+    b_out[...] = b_in[...]
+    c_out[...] = c_in[...]
 
 
 def local(video_tokens, w_query, text_keys, text_values, grad_out):
     vmem = pltpu.VMEM
-    return pl.pallas_call(
+    out_shape = (
+        jax.ShapeDtypeStruct((16, DEPTH), BF16),
+        jax.ShapeDtypeStruct((2, WIDTH), BF16),
+        jax.ShapeDtypeStruct((2, WIDTH), BF16),
+    )
+    results = pl.pallas_call(
         kernel,
-        out_shape=(
-            jax.ShapeDtypeStruct((16, DEPTH), BF16),
-            jax.ShapeDtypeStruct((2, WIDTH), BF16),
-            jax.ShapeDtypeStruct((2, WIDTH), BF16),
-        ),
+        out_shape=out_shape,
         in_specs=[pl.BlockSpec(memory_space=pl.ANY)] * 5,
         out_specs=(pl.BlockSpec(memory_space=pltpu.VMEM),) * 3,
         scratch_shapes=[
@@ -296,9 +414,10 @@
             vmem((HEADS, 4, 4, 4, ROWS, HEAD_DIM), BF16),
             vmem((HEADS, TEXT, TOKENS), F32),
             vmem((TOKENS, WIDTH), BF16),
-            vmem((2, 4, 32, WIDTH), F32),
-            vmem((3, 2, 32, WIDTH), F32),
-            vmem((3, 2, 8, WIDTH), F32),
+            vmem((4, TOKENS, CHUNK), F32),
+            vmem((2, 4, 4, 8, WIDTH), F32),
+            vmem((2, 3, 4, 8, WIDTH), F32),
+            vmem((2, 3, 8, WIDTH), F32),
             vmem((2, 4, 8, WIDTH), F32),
             vmem((4, 2, 2, WIDTH), F32),
             vmem((3, 2, 2, WIDTH), F32),
@@ -315,6 +434,12 @@
         ],
         compiler_params=pltpu.CompilerParams(collective_id=0, has_side_effects=True),
     )(video_tokens, w_query, text_keys, text_values, grad_out)
+    return pl.pallas_call(
+        hand_over,
+        out_shape=out_shape,
+        in_specs=[pl.BlockSpec(memory_space=pltpu.VMEM)] * 3,
+        out_specs=(pl.BlockSpec(memory_space=pltpu.VMEM),) * 3,
+    )(*results)
 
 
 def solution(mesh):

time: 99.6 us -> 88.4 us (0.89)
  Pallas kernels: 94.6 us -> 87.6 us
  local copies, waits for them, and re-layouts: 4.1 us -> 0 us
    pallas_call x1 -> x2, Pallas kernels: 94.6 us -> 87.6 us  [the longest x1 86 us: local(): pl.pallas_call(kernel, out_shape=out_shape, in_specs=[pl.BlockSpec(memory...]
    unnamed x3 -> x0, local copies, waits for them, and re-layouts: 4.1 us -> none
where the time goes in v2:
time: 88.4 us; the launch traced here: 88.2 us
  Pallas kernels  87.6 us (99%)
    pallas_call x1, Pallas kernels, local(): pl.pallas_call(kernel, out_shape=out_shape, in_specs=[pl.BlockSpec(memory...  86 us

profile of v2, /device:TPU:1, one launch (start us, length us, event | category | flops | bytes accessed | tf_op | source)
XLA Modules:
  0.0 88.2 jit_solution(14624085272154612953)
XLA Ops:
  0.6 86.0 %shard_map.76 = (bf16[16,5120]{1,0:T(8,128)(2,1)}, bf16[2,640]{1,0:T(2,128)(2,1)}, bf16[2,640]{1,0:T(2,128)(2,1)}) custom-call(bf16[128,5120]{1,0:T(8,128)(2,1)} %video_hbm.1, bf16[80,640]{1,0:T(8,128)(2,1)} %weight_hbm.1, bf16[128,640]{1,0:T(8,128)(2,1)} %keys_hbm.1, bf16[128,640]{1,0:T(8,128)(2,1)} %values_hbm.1, bf16[128,640]{1,0:T(8,128)(2,1)} %grad_hbm.1), custom_call_target="tpu_custom_call" | custom-call | tf_op jit(solution)/shard_map/pallas_call | solution.py:403
  86.6 1.6 %shard_map.77 = (bf16[16,5120]{1,0:T(8,128)(2,1)}, bf16[2,640]{1,0:T(2,128)(2,1)}, bf16[2,640]{1,0:T(2,128)(2,1)}) custom-call(bf16[16,5120]{1,0:T(8,128)(2,1)} %get-tuple-element.6.a_in, bf16[2,640]{1,0:T(2,128)(2,1)} %get-tuple-element.7.b_in, bf16[2,640]{1,0:T(2,128)(2,1)} %get-tuple-element.8.c_in), custom_call_target="tpu_custom_call" | custom-call | tf_op jit(solution)/shard_map/pallas_call | solution.py:437

commit v3 on v2

--- a/solution.py
+++ b/solution.py
@@ -16,7 +16,7 @@
 WIDTH = HEADS * HEAD_DIM
 AXES = ("y", "zl", "x", "zh", "c")
 SEQ = ("y", "zl", "x")
-COPIES = 126
+COPIES = 132
 F32 = jnp.float32
 BF16 = jnp.bfloat16
 
@@ -180,12 +180,11 @@
             grad_att[k] = dot(values_k, grad[:, columns(k)], (1, 1))
 
     def attention(k):
-        query = jnp.zeros((TOKENS, HEAD_DIM), F32)
-        for j in range(4):
-            query += dot(
-                video[:, j * CHUNK : (j + 1) * CHUNK], weight[k, j].reshape(CHUNK, HEAD_DIM), (1, 0)
-            )
-        query = query.astype(BF16)
+        parts = [
+            dot(video[:, j * CHUNK : (j + 1) * CHUNK], weight[k, j].reshape(CHUNK, HEAD_DIM), (1, 0))
+            for j in range(4)
+        ]
+        query = (parts[0] + parts[1] + (parts[2] + parts[3])).astype(BF16)
         keys_k = keys[:, columns(k)]
         scores = dot(keys_k, query, (1, 1)) * factor
         raised = jnp.exp(scores - jnp.max(scores, axis=0, keepdims=True))
@@ -216,8 +215,8 @@
 
     sent_if = []
 
-    def plane_send(which, go, to):
-        ref = weight.at[last, :, which]
+    def plane_send(which, half, go, to):
+        ref = weight.at[last, pl.ds(2 * half, 2), which]
         copy = mail.make(ref, ref, zl=to)
         pl.when(go)(copy.start)
         sent_if.append((copy, go))
@@ -228,10 +227,10 @@
 
     z_up, z_down = (z + 1) % 4, (z + 3) % 4
 
-    def planes(step):
+    def planes(step, half):
         lower, upper = (z + 4 - step) % 4, (z + step) % 4
-        up = plane_send(lower, jnp.logical_and(z >= step, z < 3), z_up)
-        down = plane_send(upper, jnp.logical_and(z + step <= 3, z > 0), z_down)
+        up = plane_send(lower, half, jnp.logical_and(z >= step, z < 3), z_up)
+        down = plane_send(upper, half, jnp.logical_and(z + step <= 3, z > 0), z_down)
         return up, down
 
     def planes_in(copies, step):
@@ -239,16 +238,16 @@
         plane_arrived(copies[1], z + step + 1 <= 3)
 
     prepare()
+    arrived(*a1)
+    a2 = small_a()
+    arrived(*b1)
+    b2 = small_b()
     arrived(z0[0])
     y0 = small_y(single(0))
     slices = by_x(weight.at[0, y, near_pair, x])
     arrived(*z0[1:])
     x0 = small_x(single(0))
     slices += by_y(weight.at[0, y, other_pair, x])
-    arrived(*a1)
-    a2 = small_a()
-    arrived(*b1)
-    b2 = small_b()
     arrived(*y0)
     y0_on = small_y_on(single(0))
     slices += by_x(weight.at[0, yn, near_pair, x]) + by_x(weight.at[0, yp, near_pair, x])
@@ -277,7 +276,7 @@
     arrived(*z2[1:])
     x2 = small_x(double)
     arrived(a2_on, b2_on)
-    plane[0] = planes(0)
+    plane[0] = planes(0, 0), planes(0, 1)
     arrived(*y1_on)
     big[1] = big_x(1)
     arrived(*x1_on)
@@ -288,32 +287,38 @@
     x2_on = small_x_on(double)
     arrived(*slices)
     big_done[0] = big_on(0)
+    planes_in(plane[0][0], 0)
+    plane[1] = [planes(1, 0)]
     arrived(*y2_on, *x2_on)
     big[2] = big_x(2) + big_y(2)
     arrived(*big[1])
     big_done[1] = big_on(1)
     big[3] = big_x(3) + big_y(3)
-    planes_in(plane[0], 0)
-    plane[1] = planes(1)
+    planes_in(plane[0][1], 0)
+    plane[1] += [planes(1, 1)]
     arrived(*big_done[0])
+    planes_in(plane[1][0], 1)
+    plane[2] = [planes(2, 0)]
     attention(0)
     gather_back(0)
     arrived(*big[2])
     big_done[2] = big_on(2)
     arrived(*big_done[1])
+    planes_in(plane[1][1], 1)
+    plane[2] += [planes(2, 1)]
     attention(1)
     gather_back(1)
-    planes_in(plane[1], 1)
-    plane[2] = planes(2)
     arrived(*big[3])
     big_done[3] = big_on(3)
     arrived(*big_done[2])
     attention(2)
     gather_back(2)
+    planes_in(plane[2][0], 2)
+    planes_in(plane[2][1], 2)
+    attention(4)
+    gather_back(4)
     arrived(*big_done[3])
-    planes_in(plane[2], 2)
     attention(3)
-    attention(4)
 
     key_in = [mail.send(kv.at[0, to], kv_1.at[0, n], x=to) for n, to in enumerate((xp, xn, xf))]
     value_in = [mail.send(kv.at[1, :, to], kv_1.at[1, n], y=to) for n, to in enumerate((yp, yn, yf))]
@@ -322,7 +327,7 @@
     pair_in, far_in, up_in, down_in = {}, {}, {}, {}
 
     def make_part(j):
-        whole = (made[j] + back(3, j) + back(4, j)).astype(BF16)
+        whole = (made[j] + back(3, j)).astype(BF16)
         for t in range(8):
             part[j, t % 2, t // 2] = whole[t * 16 : (t + 1) * 16]
         pair_in[j] = mail.send(part.at[j, 1 - c], part_in.at[j], c=1 - c)

time: 88.4 us -> 86.9 us (0.983)
  Pallas kernels: 87.6 us -> 85.9 us
    pallas_call x1, Pallas kernels: 86 us -> 84.3 us  [local(): pl.pallas_call(kernel, out_shape=out_shape, in_specs=[pl.BlockSpec(memory...]
where the time goes in v3:
time: 86.9 us; the launch traced here: 86.5 us
  Pallas kernels  85.9 us (99%)
    pallas_call x1, Pallas kernels, local(): pl.pallas_call(kernel, out_shape=out_shape, in_specs=[pl.BlockSpec(memory...  84.3 us

profile of v3, /device:TPU:1, one launch (start us, length us, event | category | flops | bytes accessed | tf_op | source)
XLA Modules:
  0.0 86.5 jit_solution(8549484277018535756)
XLA Ops:
  0.6 84.3 %shard_map.76 = (bf16[16,5120]{1,0:T(8,128)(2,1)}, bf16[2,640]{1,0:T(2,128)(2,1)}, bf16[2,640]{1,0:T(2,128)(2,1)}) custom-call(bf16[128,5120]{1,0:T(8,128)(2,1)} %video_hbm.1, bf16[80,640]{1,0:T(8,128)(2,1)} %weight_hbm.1, bf16[128,640]{1,0:T(8,128)(2,1)} %keys_hbm.1, bf16[128,640]{1,0:T(8,128)(2,1)} %values_hbm.1, bf16[128,640]{1,0:T(8,128)(2,1)} %grad_hbm.1), custom_call_target="tpu_custom_call" | custom-call | tf_op jit(solution)/shard_map/pallas_call | solution.py:408
  84.9 1.6 %shard_map.77 = (bf16[16,5120]{1,0:T(8,128)(2,1)}, bf16[2,640]{1,0:T(2,128)(2,1)}, bf16[2,640]{1,0:T(2,128)(2,1)}) custom-call(bf16[16,5120]{1,0:T(8,128)(2,1)} %get-tuple-element.6.a_in, bf16[2,640]{1,0:T(2,128)(2,1)} %get-tuple-element.7.b_in, bf16[2,640]{1,0:T(2,128)(2,1)} %get-tuple-element.8.c_in), custom_call_target="tpu_custom_call" | custom-call | tf_op jit(solution)/shard_map/pallas_call | solution.py:442

commit v4 on v3

--- a/solution.py
+++ b/solution.py
@@ -323,6 +323,7 @@
     key_in = [mail.send(kv.at[0, to], kv_1.at[0, n], x=to) for n, to in enumerate((xp, xn, xf))]
     value_in = [mail.send(kv.at[1, :, to], kv_1.at[1, n], y=to) for n, to in enumerate((yp, yn, yf))]
 
+    gathered = len(mail.sent)
     order = (0, 2, 1, 3)
     pair_in, far_in, up_in, down_in = {}, {}, {}, {}
 
@@ -376,6 +377,10 @@
     send_on(1)
     send_on(3)
 
+    for copy in mail.sent[:gathered]:
+        copy.wait_send()
+    for copy, go in sent_if:
+        pl.when(go)(copy.wait_send)
     for j in order:
         arrived(up_in[j], down_in[j])
         out_video[:, j * CHUNK : (j + 1) * CHUNK] = (
@@ -386,10 +391,8 @@
     out_keys[...] = both[0].astype(BF16)
     out_values[...] = both[1].astype(BF16)
     assert len(mail.made) == COPIES, len(mail.made)
-    for copy in mail.sent:
+    for copy in mail.sent[gathered:]:
         copy.wait_send()
-    for copy, go in sent_if:
-        pl.when(go)(copy.wait_send)
 
 
 def hand_over(a_in, b_in, c_in, a_out, b_out, c_out):

time: 86.9 us -> 86.7 us (level)
  no operation moved by 1% of the time
where the time goes in v4:
time: 86.7 us; the launch traced here: 86.3 us
  Pallas kernels  85.7 us (99%)
    pallas_call x1, Pallas kernels, local(): pl.pallas_call(kernel, out_shape=out_shape, in_specs=[pl.BlockSpec(memory...  84.1 us

profile of v4, /device:TPU:1, one launch (start us, length us, event | category | flops | bytes accessed | tf_op | source)
XLA Modules:
  0.0 86.3 jit_solution(17152387643972665064)
XLA Ops:
  0.6 84.1 %shard_map.76 = (bf16[16,5120]{1,0:T(8,128)(2,1)}, bf16[2,640]{1,0:T(2,128)(2,1)}, bf16[2,640]{1,0:T(2,128)(2,1)}) custom-call(bf16[128,5120]{1,0:T(8,128)(2,1)} %video_hbm.1, bf16[80,640]{1,0:T(8,128)(2,1)} %weight_hbm.1, bf16[128,640]{1,0:T(8,128)(2,1)} %keys_hbm.1, bf16[128,640]{1,0:T(8,128)(2,1)} %values_hbm.1, bf16[128,640]{1,0:T(8,128)(2,1)} %grad_hbm.1), custom_call_target="tpu_custom_call" | custom-call | tf_op jit(solution)/shard_map/pallas_call | solution.py:411
  84.7 1.6 %shard_map.77 = (bf16[16,5120]{1,0:T(8,128)(2,1)}, bf16[2,640]{1,0:T(2,128)(2,1)}, bf16[2,640]{1,0:T(2,128)(2,1)}) custom-call(bf16[16,5120]{1,0:T(8,128)(2,1)} %get-tuple-element.6.a_in, bf16[2,640]{1,0:T(2,128)(2,1)} %get-tuple-element.7.b_in, bf16[2,640]{1,0:T(2,128)(2,1)} %get-tuple-element.8.c_in), custom_call_target="tpu_custom_call" | custom-call | tf_op jit(solution)/shard_map/pallas_call | solution.py:445
